TPU v7x, 256 devices: a whole 4x4x8 slice. The times are simulated.
256 devices in a mesh: wide: 32 (over y, x, core), narrow: 8 (over z).
Axes of the slice: x: 4, y: 4, z: 8, core: 2. Of those that a mesh axis runs over, the one named last changes fastest.
Arguments:
- thinker_rows: bfloat16 [32, 8, 3, 2, 128, 2048], P('wide', 'narrow'), may hold values from -6 to 6
- codec_ids: int32 [32, 8, 3, 2, 128], P('wide', 'narrow'), may hold values from 0 to 2047
- block_lengths: int32 [32, 8, 3, 2], P('wide', 'narrow'), may hold values from 1 to 128
- chosen_label: int32 [32, 8, 3], P('wide', 'narrow'), may hold values from 0 to 1
- ref_logratio: float32 [32, 8, 3], P('wide', 'narrow'), may hold values from -6 to 6
- pair_count: int32 [32, 8], P('wide', 'narrow'), may hold values from 1 to 3, as said below
- proj_weight: bfloat16 [2048, 1024], P('narrow'), may hold values from -0.125 to 0.125
- norm_gain: bfloat16 [1024], P('narrow'), may hold values from 0.25 to 1.75
- head_weight: bfloat16 [1024, 2048], P('narrow')
Outputs:
- loss: float32 [], replicated
- grad_head: float32 [1024, 2048], P('narrow')
- grad_gain: float32 [1024], P('narrow')
Inputs may be any that keep to these rules, and one draw needn't show every extreme that they name: `pair_count`: owners are ordered with the wide index slowest; the counts sum to 512; the sum of the counts of owners below owner i lies between i * 2 and i * 2 + 1; some owner holds 3 live pairs.
All inputs are finite; a program needn't handle non-finite values.
Results may differ from a plain program's by a relative error of at most 0.017.
The roundings to bfloat16 on the way count: a program that leaves them out, or rounds other values in their place, can miss the bound.
Values may be sent and summed in bfloat16 or wider, within the bound.
No kernel may reach another device: no remote copies, remote signals or barrier semaphores. Data moves between devices by JAX's collectives and lax.ppermute only.
A program may use at most 64 MiB of HBM per device.

v0:
```python
import jax
import jax.numpy as jnp
from jax import lax
from jax.sharding import PartitionSpec as P

norm_eps = 1e-06
margin_scale = 2.0


def forward_terms(projected, codes, lengths, live_pairs, gain_full, head_full):
    pairs = codes.shape[0]
    frames = codes.shape[2]
    flat = projected.astype(jnp.float32)
    inverse = lax.rsqrt(jnp.mean(flat * flat, axis=1, keepdims=True) + norm_eps)
    normed = (flat * inverse * gain_full.astype(jnp.float32)).astype(jnp.bfloat16)
    logits = jnp.dot(normed, head_full, preferred_element_type=jnp.float32)
    highest = jnp.max(logits, axis=1, keepdims=True)
    log_total = highest + jnp.log(jnp.sum(jnp.exp(logits - highest), axis=1, keepdims=True))
    probs = jnp.exp(logits - log_total)
    target = (lax.broadcasted_iota(jnp.int32, logits.shape, 1) == codes.reshape(-1, 1)).astype(
        jnp.float32
    )
    token_logp = jnp.sum(target * logits, axis=1) - log_total[:, 0]
    frame_index = jnp.arange(frames, dtype=jnp.int32)
    valid = ((frame_index[None, None, :] < lengths[:, :, None]) & live_pairs[:, None, None]).astype(
        jnp.float32
    )
    partial_value = jnp.sum(token_logp.reshape(pairs, 2, frames) * valid, axis=2)
    return (normed, flat, inverse, probs, target, valid, partial_value)


def backward_terms(
    scores, lengths, labels, ratios, live_pairs, flat, inverse, probs, target, valid, head_full
):
    length_f = lengths.astype(jnp.float32)
    score = scores / length_f
    first = labels == 0
    chosen = jnp.where(first, score[:, 0], score[:, 1])
    rejected = jnp.where(first, score[:, 1], score[:, 0])
    margin = margin_scale * (chosen - rejected - ratios)
    live_f = live_pairs.astype(jnp.float32)
    loss_part = jnp.sum(jax.nn.softplus(-margin) * live_f)
    slope = -jax.nn.sigmoid(-margin) * live_f
    weight_first = jnp.where(first, margin_scale * slope, -margin_scale * slope)
    block_weight = jnp.stack([weight_first, -weight_first], axis=1) / length_f
    coeff = (block_weight[:, :, None] * valid).reshape(-1, 1)
    dlogits = (coeff * (target - probs)).astype(jnp.bfloat16)
    dnormed = jnp.dot(dlogits, head_full.T, preferred_element_type=jnp.float32)
    gain_term = jnp.sum(dnormed * flat * inverse, axis=0)
    return (loss_part, dlogits, gain_term)


def on_device(
    thinker_rows,
    codec_ids,
    block_lengths,
    chosen_label,
    ref_logratio,
    pair_count,
    proj_weight,
    norm_gain,
    head_weight,
):
    slots = thinker_rows.shape[2]
    frames = thinker_rows.shape[4]
    thinker_width = thinker_rows.shape[5]
    width = proj_weight.shape[1]
    hold = (slots + 1) // 2
    wide_count = lax.axis_size("wide")
    narrow_count = lax.axis_size("narrow")
    flat_rows = thinker_rows.reshape(slots * 2 * frames, thinker_width)
    projected = jnp.dot(
        flat_rows,
        lax.all_gather(proj_weight, "narrow", axis=0, tiled=True),
        preferred_element_type=jnp.float32,
    ).astype(jnp.bfloat16)
    head_full, gain_full = (
        lax.all_gather(head_weight, "narrow", axis=0, tiled=True),
        lax.all_gather(norm_gain, "narrow", axis=0, tiled=True),
    )
    codes = codec_ids[0, 0]
    lengths = block_lengths[0, 0]
    labels = chosen_label[0, 0]
    ratios = ref_logratio[0, 0]
    live_pairs = jnp.arange(slots, dtype=jnp.int32) < pair_count[0, 0]
    normed, flat, inverse, probs, target, valid, partial_value = forward_terms(
        projected, codes, lengths, live_pairs, gain_full, head_full
    )
    loss_part, dlogits, gain_term = backward_terms(
        partial_value,
        lengths,
        labels,
        ratios,
        live_pairs,
        flat,
        inverse,
        probs,
        target,
        valid,
        head_full,
    )
    pair_total = wide_count * narrow_count * hold
    loss_sum = lax.psum(loss_part, ("wide", "narrow"))
    block = width // (wide_count * narrow_count)
    row_count = normed.shape[0]
    normed_order = (
        normed.reshape(row_count, narrow_count, wide_count, block)
        .transpose(0, 2, 1, 3)
        .reshape(row_count, width)
    )
    head_order = jnp.dot(normed_order.T, dlogits, preferred_element_type=jnp.float32)
    gain_order = (
        gain_term.reshape(narrow_count, wide_count, block).transpose(1, 0, 2).reshape(width)
    )
    head_piece, gain_piece = (
        lax.psum_scatter(head_order, ("wide", "narrow"), scatter_dimension=0, tiled=True),
        lax.psum_scatter(gain_order, ("wide", "narrow"), scatter_dimension=0, tiled=True),
    )
    grad_head, grad_gain = (
        lax.all_gather(head_piece.astype(jnp.bfloat16), "wide", axis=0, tiled=True).astype(
            head_piece.dtype
        ),
        lax.all_gather(gain_piece.astype(jnp.bfloat16), "wide", axis=0, tiled=True).astype(
            gain_piece.dtype
        ),
    )
    return (loss_sum / pair_total, grad_head, grad_gain)


def solution(mesh):
    in_specs = (
        P("wide", "narrow", None, None, None, None),
        P("wide", "narrow", None, None, None),
        P("wide", "narrow", None, None),
        P("wide", "narrow", None),
        P("wide", "narrow", None),
        P("wide", "narrow"),
        P("narrow", None),
        P("narrow"),
        P("narrow", None),
    )
    out_specs = (P(), P("narrow", None), P("narrow"))
    return jax.shard_map(
        on_device, mesh=mesh, in_specs=in_specs, out_specs=out_specs, check_vma=False
    )
```

profile of v0, /device:TPU:1, one launch (start us, length us, event | category | flops | bytes accessed | tf_op | source)
XLA Modules:
  0.0 399.8 jit_solution(17206909398932565671)
XLA Ops:
  7.2 0.0 copy-start
  7.2 0.0 all-gather.5.cloned.1.call-start
  7.2 0.7 all-gather.5.cloned.1.call-update
  7.9 0.0 all-gather.7.cloned.1.call-start
  8.0 0.7 all-gather.7.cloned.1.call-update
  9.3 0.7 compare_bitcast_fusion
  10.0 0.1 copy.40
  10.1 0.8 copy.33
  10.9 0.7 copy.39
  11.6 0.7 eq.29
  12.3 16.4 %all-gather = bf16[8,1,128]{2,1,0:T(2,128)(2,1)S(1)} all-gather(bf16[1,1,128]{2,1,0:T(2,128)(2,1)} %bitcast.53), channel_id=1, replica_groups=mesh['wide'=32,'narrow'=8] {'narrow'}, dimensions={0}, use_global_device_ids=true | all-gather | bytes 2304 | tf_op jit(solution)/shard_map/all_gather | solution.py:79
  28.7 1.3 dynamic-slice
  29.9 38.3 %all-gather.5.cloned.1.call-done = bf16[2048,1024]{1,0:T(8,128)(2,1)} async-done(((bf16[256,1024]{1,0:T(8,128)(2,1)}), bf16[2048,1024]{1,0:T(8,128)(2,1)}) %all-gather.5.cloned.1.call-update) | async-done | bytes 4194320 | tf_op jit(solution)/shard_map/all_gather | solution.py:74
  68.2 0.0 copy-done
  68.2 5.7 %fusion = (f32[768]{0:T(1024)S(1)}, bf16[768,1024]{1,0:T(8,128)(2,1)S(1)}) fusion(bf16[768,2048]{1,0:T(8,128)(2,1)S(1)} %bitcast.47, bf16[2048,1024]{1,0:T(8,128)(2,1)} %all-gather.5.cloned.1.call-done), kind=kOutput, calls=%fused_computation.7 | convolution fusion | flops 3224370432 | bytes 8915968 | tf_op jit(solution)/shard_map/dot_general | solution.py:72
  73.9 0.0 copy-start.3
  73.9 1.1 copy-done.3
  75.0 1.6 fusion.2
  76.6 2.6 copy.35
  79.2 3.9 reshape.130
  83.1 3.4 copy.36
  86.5 3.8 reshape.131
  90.3 33.1 %all-gather.7.cloned.1.call-done = bf16[1024,2048]{1,0:T(8,128)(2,1)} async-done(((bf16[128,2048]{1,0:T(8,128)(2,1)}), bf16[1024,2048]{1,0:T(8,128)(2,1)}) %all-gather.7.cloned.1.call-update) | async-done | bytes 4194320 | tf_op jit(solution)/shard_map/all_gather | solution.py:78
  123.4 5.8 %fusion.13 = (f32[768]{0:T(1024)S(1)}, f32[768,2048]{1,0:T(8,128)S(1)}) fusion(bf16[768,1024]{1,0:T(8,128)(2,1)} %fusion.2, bf16[1024,2048]{1,0:T(8,128)(2,1)} %all-gather.7.cloned.1.call-done), kind=kOutput, calls=%fused_computation.38 | convolution fusion | flops 3222797568 | bytes 12061696 | tf_op jit(solution)/shard_map/dot_general | solution.py:16
  129.2 0.0 copy-start.1
  129.2 2.0 exponential_reduce_fusion
  131.2 0.7 copy-done.1
  131.8 0.2 select_reduce_fusion.1
  132.0 0.2 fusion.11
  132.2 0.1 maximum_divide_fusion
  132.3 0.1 fusion.6
  132.4 0.0 copy-start.4
  132.4 0.0 copy-start.7
  132.4 4.4 %multiply_convert_fusion = bf16[768,2048]{1,0:T(8,128)(2,1)S(1)} fusion(f32[768,2048]{1,0:T(8,128)} %copy-done.1, f32[768]{0:T(1024)S(1)} %get-tuple-element.13, f32[768]{0:T(1024)S(1)} %mul.90, s32[768]{0:T(1024)S(1)} %eq.29), kind=kLoop, calls=%fused_computation | loop fusion | flops 9437184 | bytes 9446400 | tf_op jit(solution)/shard_map/convert_element_type | solution.py:47
  136.9 0.0 copy-start.2
  136.9 1.7 copy-done.2
  138.6 0.0 copy-done.4
  138.6 0.0 copy-done.7
  138.6 3.5 fusion.4
  142.1 0.1 reshape.132
  142.3 0.1 copy.41
  142.4 0.1 reshape.133
  142.5 0.0 copy-start.5
  142.5 0.0 copy-start.6
  142.5 9.0 %fusion.14 = f32[1024,2048]{1,0:T(8,128)} fusion(bf16[768,1024]{0,1:T(8,128)(2,1)} %reshape.131, bf16[768,2048]{1,0:T(8,128)(2,1)} %copy-done.2), kind=kOutput, calls=%fused_computation.39 | convolution fusion | flops 3221225472 | bytes 13107200 | tf_op jit(solution)/shard_map/dot_general | solution.py:111
  151.5 0.0 copy-done.5
  151.5 0.0 copy-done.6
  151.5 0.6 fusion.10
  152.8 144.7 %all-reduce.5 = (f32[]{:T(128)}, bf16[1024,2048]{1,0:T(8,128)(2,1)}, bf16[1024]{0:T(1024)(128)(2,1)S(1)}) all-reduce(f32[]{:T(128)} %fusion.10, f32[1024,2048]{1,0:T(8,128)} %fusion.14, f32[1024]{0:T(1024)S(1)} %reshape.133), channel_id=1, replica_groups=mesh['wide'=32,'narrow'=8] {'wide','narrow'}, use_global_device_ids=true, to_apply=%region_6.7 | all-reduce | flops 2098177 | bytes 12589064 | tf_op jit(solution)/shard_map/psum | solution.py:103
  297.5 0.8 fusion.5
  298.3 0.1 dynamic-slice.7
  298.4 0.2 dynamic-update-slice
  298.6 64.9 %all-reduce = bf16[128]{0:T(256)(128)(2,1)S(1)} all-reduce(bf16[128]{0:T(256)(128)(2,1)S(1)} %dynamic-update-slice), channel_id=1, replica_groups=mesh['wide'=32,'narrow'=8] {'wide'}, use_global_device_ids=true, to_apply=%add | all-reduce | flops 128 | bytes 512
  363.5 0.5 convert_element_type.49
  364.0 25.1 %all-gather.1 = bf16[32,4,2048]{2,1,0:T(4,128)(2,1)} all-gather(bf16[1,4,2048]{2,1,0:T(4,128)(2,1)S(1)} %fusion.5), channel_id=1, replica_groups=mesh['wide'=32,'narrow'=8] {'wide'}, dimensions={0}, use_global_device_ids=true | all-gather | bytes 540672 | tf_op jit(solution)/shard_map/all_gather | solution.py:120
  389.1 2.1 reshape.142
  (8 shorter events, 0.1 us)
Async XLA Ops:
  7.2 61.1 %copy-start = (bf16[1,1,3,2,128,2048]{5,4,3,2,1,0:T(8,128)(2,1)S(1)}, bf16[1,1,3,2,128,2048]{5,4,3,2,1,0:T(8,128)(2,1)}, u32[]{:S(2)}) copy-start(bf16[1,1,3,2,128,2048]{5,4,3,2,1,0:T(8,128)(2,1)} %param.9) | copy-start | bytes 9437188
  7.2 61.0 %all-gather.5.cloned.1.call-start = ((), (), s32[]{:S(2)}) async-start(), calls=%async_computation | async-start | bytes 4718592 | tf_op jit(solution)/shard_map/all_gather | solution.py:74
  7.9 115.4 %all-gather.7.cloned.1.call-start = ((), (), s32[]{:S(2)}) async-start(), calls=%async_computation.1 | async-start | bytes 4718592 | tf_op jit(solution)/shard_map/all_gather | solution.py:78
  73.9 1.2 copy-start.3
  129.2 2.7 copy-start.1
  132.4 6.2 %copy-start.4 = (bf16[768,1024]{1,0:T(8,128)(2,1)S(1)}, bf16[768,1024]{1,0:T(8,128)(2,1)}, u32[]{:S(2)}) copy-start(bf16[768,1024]{1,0:T(8,128)(2,1)} %copy-done.3) | copy-start | bytes 4718596
  132.4 6.2 %copy-start.7 = (bf16[1024,2048]{1,0:T(8,128)(2,1)S(1)}, bf16[1024,2048]{1,0:T(8,128)(2,1)}, u32[]{:S(2)}) copy-start(bf16[1024,2048]{1,0:T(8,128)(2,1)} %all-gather.7.cloned.1.call-done) | copy-start | bytes 12582916
  136.9 1.8 copy-start.2
  142.5 9.0 %copy-start.5 = (f32[1,1,3]{2,1,0:T(1,128)S(1)}, f32[1,1,3]{2,1,0:T(1,128)}, u32[]{:S(2)}) copy-start(f32[1,1,3]{2,1,0:T(1,128)} %param.13) | copy-start | bytes 40
  142.5 9.0 %copy-start.6 = (s32[1,1,3]{2,1,0:T(1,128)S(1)}, s32[1,1,3]{2,1,0:T(1,128)}, u32[]{:S(2)}) copy-start(s32[1,1,3]{2,1,0:T(1,128)} %param.12) | copy-start | bytes 40
Sparse Core Ops, SparseCore 0:
  9.8 58.3 all-gather.4
  70.0 53.3 all-gather.6
where the time goes:
time: 400 us
  blocking collectives  251 us (63%)
  waiting for transfers between devices  72.7 us (18%)
  local copies, waits for them, and re-layouts  24.3 us (6%)
  matrix products  24 us (6%)
  between operations  17.3 us (4%)
  other arithmetic  10.3 us (3%)
    psum x1, blocking collectives, on_device(): loss_sum = lax.psum(loss_part, ('wide', 'narrow'))  145 us
    unnamed x1, blocking collectives  64.9 us
    all_gather x1, waiting for transfers between devices, on_device(): lax.all_gather(proj_weight, 'narrow', axis=0, tiled=True)  38.3 us
    all_gather x1, waiting for transfers between devices, on_device(): lax.all_gather(head_weight, 'narrow', axis=0, tiled=True)  33.1 us
    all_gather x1, blocking collectives, on_device(): lax.all_gather(head_piece.astype(jnp.bfloat16), 'wide', axis=0, tiled=True)  25.1 us
    all_gather x1, blocking collectives, on_device(): lax.all_gather(norm_gain, 'narrow', axis=0, tiled=True)  16.4 us
    dot_general x1, matrix products, on_device(): jnp.dot(normed_order.T, dlogits, preferred_element_type=jnp.float32)  9.01 us
  transfers between devices with their start and end apart: 2, of which 2 were waited for; matrix products, arithmetic and copies ran while one was open for 6% of the time, Pallas kernels for 0%

commit v1 on v0

--- a/solution.py
+++ b/solution.py
@@ -117,9 +117,12 @@
         lax.psum_scatter(gain_order, ("wide", "narrow"), scatter_dimension=0, tiled=True),
     )
     grad_head, grad_gain = (
-        lax.all_gather(head_piece.astype(jnp.bfloat16), "wide", axis=0, tiled=True).astype(
-            head_piece.dtype
-        ),
+        jnp.concatenate(
+            lax.all_to_all(
+                jnp.stack([head_piece.astype(jnp.bfloat16)] * lax.axis_size("wide")), "wide", 0, 0
+            ),
+            axis=0,
+        ).astype(head_piece.dtype),
         lax.all_gather(gain_piece.astype(jnp.bfloat16), "wide", axis=0, tiled=True).astype(
             gain_piece.dtype
         ),

time: 400 us -> 385 us (0.963)
  blocking collectives: 251 us -> 225 us
  starting transfers between devices: 0.08 us -> 7.13 us
    all_gather x1 -> x0, blocking collectives: 25.1 us -> none  [on_device(): lax.all_gather(head_piece.astype(jnp.bfloat16), 'wide', axis=0, tiled=True)]
    all_to_all x0 -> x1, starting transfers between devices: none -> 7.05 us  [on_device(): lax.all_to_all(jnp.stack([head_piece.astype(jnp.bfloat16)] * lax.axis_siz...]
  transfers between devices with their start and end apart: 2 -> 3, of which waited for: 2 -> 2; matrix products, arithmetic and copies ran while one was open for 6% -> 7% of each run, Pallas kernels for 0% -> 0%
where the time goes in v1:
time: 385 us; the launch traced here: 383 us
  blocking collectives  225 us (58%)
  waiting for transfers between devices  74 us (19%)
  local copies, waits for them, and re-layouts  24.6 us (6%)
  matrix products  24 us (6%)
  between operations  17.3 us (4%)
  other arithmetic  10.3 us (3%)
  starting transfers between devices  7.13 us (2%)
    psum x1, blocking collectives, on_device(): loss_sum = lax.psum(loss_part, ('wide', 'narrow'))  145 us
    unnamed x1, blocking collectives  64.3 us
    all_gather x1, waiting for transfers between devices, on_device(): lax.all_gather(proj_weight, 'narrow', axis=0, tiled=True)  39.5 us
    all_gather x1, waiting for transfers between devices, on_device(): lax.all_gather(head_weight, 'narrow', axis=0, tiled=True)  33.1 us
    all_gather x1, blocking collectives, on_device(): lax.all_gather(norm_gain, 'narrow', axis=0, tiled=True)  16.4 us
    dot_general x1, matrix products, on_device(): jnp.dot(normed_order.T, dlogits, preferred_element_type=jnp.float32)  9.01 us
  transfers between devices with their start and end apart: 3, of which 2 were waited for; matrix products, arithmetic and copies ran while one was open for 7% of the time, Pallas kernels for 0%

profile of v1, /device:TPU:1, one launch (start us, length us, event | category | flops | bytes accessed | tf_op | source)
XLA Modules:
  0.0 382.7 jit_solution(4015921430239310383)
XLA Ops:
  7.2 0.0 copy-start
  7.2 0.0 all-gather.4.cloned.1.call-start
  7.2 0.7 all-gather.4.cloned.1.call-update
  7.9 0.0 all-gather.6.cloned.1.call-start
  8.0 0.7 all-gather.6.cloned.1.call-update
  9.3 0.7 compare_bitcast_fusion
  10.0 0.1 copy.40
  10.1 0.8 copy.33
  10.9 0.7 copy.39
  11.6 0.7 eq.29
  12.3 16.4 %all-gather = bf16[8,1,128]{2,1,0:T(2,128)(2,1)S(1)} all-gather(bf16[1,1,128]{2,1,0:T(2,128)(2,1)} %bitcast.51), channel_id=1, replica_groups=mesh['wide'=32,'narrow'=8] {'narrow'}, dimensions={0}, use_global_device_ids=true | all-gather | bytes 2304 | tf_op jit(solution)/shard_map/all_gather | solution.py:79
  28.7 39.5 %all-gather.4.cloned.1.call-done = bf16[2048,1024]{1,0:T(8,128)(2,1)} async-done(((bf16[256,1024]{1,0:T(8,128)(2,1)}), bf16[2048,1024]{1,0:T(8,128)(2,1)}) %all-gather.4.cloned.1.call-update) | async-done | bytes 4194320 | tf_op jit(solution)/shard_map/all_gather | solution.py:74
  68.2 0.0 copy-done
  68.2 5.7 %fusion = (f32[768]{0:T(1024)S(1)}, bf16[768,1024]{1,0:T(8,128)(2,1)S(1)}) fusion(bf16[768,2048]{1,0:T(8,128)(2,1)S(1)} %bitcast.45, bf16[2048,1024]{1,0:T(8,128)(2,1)} %all-gather.4.cloned.1.call-done), kind=kOutput, calls=%fused_computation.7 | convolution fusion | flops 3224370432 | bytes 8915968 | tf_op jit(solution)/shard_map/dot_general | solution.py:72
  73.9 0.0 copy-start.3
  73.9 1.1 copy-done.3
  75.0 1.6 fusion.2
  76.6 2.6 copy.35
  79.2 3.9 %reshape.135 = bf16[768,8,32,4]{0,3,2,1:T(4,128)(2,1)} reshape(bf16[768,1024]{0,1:T(8,128)(2,1)} %copy.35) | data formatting | bytes 3145728 | tf_op jit(solution)/shard_map/reshape | solution.py:107
  83.1 3.4 copy.36
  86.5 3.8 reshape.136
  90.3 33.1 %all-gather.6.cloned.1.call-done = bf16[1024,2048]{1,0:T(8,128)(2,1)} async-done(((bf16[128,2048]{1,0:T(8,128)(2,1)}), bf16[1024,2048]{1,0:T(8,128)(2,1)}) %all-gather.6.cloned.1.call-update) | async-done | bytes 4194320 | tf_op jit(solution)/shard_map/all_gather | solution.py:78
  123.4 5.8 %fusion.12 = (f32[768]{0:T(1024)S(1)}, f32[768,2048]{1,0:T(8,128)S(1)}) fusion(bf16[768,1024]{1,0:T(8,128)(2,1)} %fusion.2, bf16[1024,2048]{1,0:T(8,128)(2,1)} %all-gather.6.cloned.1.call-done), kind=kOutput, calls=%fused_computation.37 | convolution fusion | flops 3222797568 | bytes 12061696 | tf_op jit(solution)/shard_map/dot_general | solution.py:16
  129.2 0.0 copy-start.1
  129.2 2.0 exponential_reduce_fusion
  131.2 0.7 copy-done.1
  131.8 0.2 select_reduce_fusion.1
  132.0 0.2 fusion.10
  132.2 0.1 maximum_divide_fusion
  132.3 0.1 fusion.5
  132.4 0.0 copy-start.4
  132.4 0.0 copy-start.7
  132.4 4.4 %multiply_convert_fusion = bf16[768,2048]{1,0:T(8,128)(2,1)S(1)} fusion(f32[768,2048]{1,0:T(8,128)} %copy-done.1, f32[768]{0:T(1024)S(1)} %get-tuple-element.13, f32[768]{0:T(1024)S(1)} %mul.90, s32[768]{0:T(1024)S(1)} %eq.29), kind=kLoop, calls=%fused_computation | loop fusion | flops 9437184 | bytes 9446400 | tf_op jit(solution)/shard_map/convert_element_type | solution.py:47
  136.9 0.0 copy-start.2
  136.9 1.7 copy-done.2
  138.6 0.0 copy-done.4
  138.6 0.0 copy-done.7
  138.6 3.5 fusion.4
  142.1 0.1 reshape.137
  142.3 0.1 copy.41
  142.4 0.1 reshape.138
  142.5 0.0 copy-start.5
  142.5 0.0 copy-start.6
  142.5 9.0 %fusion.13 = f32[1024,2048]{1,0:T(8,128)} fusion(bf16[768,1024]{0,1:T(8,128)(2,1)} %reshape.136, bf16[768,2048]{1,0:T(8,128)(2,1)} %copy-done.2), kind=kOutput, calls=%fused_computation.38 | convolution fusion | flops 3221225472 | bytes 13107200 | tf_op jit(solution)/shard_map/dot_general | solution.py:111
  151.5 0.0 copy-done.5
  151.5 0.0 copy-done.6
  151.5 0.6 fusion.9
  152.1 0.0 copy-start.8
  152.1 144.7 %all-reduce.5 = (f32[]{:T(128)}, bf16[1024,2048]{1,0:T(8,128)(2,1)}, bf16[1024]{0:T(1024)(128)(2,1)S(1)}) all-reduce(f32[]{:T(128)} %fusion.9, f32[1024,2048]{1,0:T(8,128)} %fusion.13, f32[1024]{0:T(1024)S(1)} %reshape.138), channel_id=1, replica_groups=mesh['wide'=32,'narrow'=8] {'wide','narrow'}, use_global_device_ids=true, to_apply=%region_6.7 | all-reduce | flops 2098177 | bytes 12589064 | tf_op jit(solution)/shard_map/psum | solution.py:103
  296.9 0.8 dynamic-slice_convert_fusion
  297.6 1.0 stack.5
  298.7 7.1 %all-to-all-start = ((bf16[32,4,2048]{2,1,0:T(4,128)(2,1)}), bf16[32,4,2048]{2,1,0:T(4,128)(2,1)}, u32[]{:S(2)}, u32[]{:S(2)}) async-start(bf16[32,4,2048]{2,1,0:T(4,128)(2,1)} %stack.5), calls=%async_computation | async-start | bytes 1048576 | tf_op jit(solution)/shard_map/all_to_all | solution.py:121
  305.7 0.0 copy-done.8
  305.7 0.6 dynamic-slice
  307.0 0.1 dynamic-slice.5
  307.1 0.2 dynamic-update-slice
  307.2 64.3 %all-reduce = bf16[128]{0:T(256)(128)(2,1)S(1)} all-reduce(bf16[128]{0:T(256)(128)(2,1)S(1)} %dynamic-update-slice), channel_id=1, replica_groups=mesh['wide'=32,'narrow'=8] {'wide'}, use_global_device_ids=true, to_apply=%add | all-reduce | flops 128 | bytes 512
  371.5 0.5 convert_element_type.53
  372.7 0.0 all-to-all-done
  372.7 2.1 reshape.139
  (8 shorter events, 0.1 us)
Async XLA Ops:
  7.2 61.1 %copy-start = (bf16[1,1,3,2,128,2048]{5,4,3,2,1,0:T(8,128)(2,1)S(1)}, bf16[1,1,3,2,128,2048]{5,4,3,2,1,0:T(8,128)(2,1)}, u32[]{:S(2)}) copy-start(bf16[1,1,3,2,128,2048]{5,4,3,2,1,0:T(8,128)(2,1)} %param.9) | copy-start | bytes 9437188
  7.2 61.0 %all-gather.4.cloned.1.call-start = ((), (), s32[]{:S(2)}) async-start(), calls=%async_computation.1 | async-start | bytes 4718592 | tf_op jit(solution)/shard_map/all_gather | solution.py:74
  7.9 115.4 %all-gather.6.cloned.1.call-start = ((), (), s32[]{:S(2)}) async-start(), calls=%async_computation.2 | async-start | bytes 4718592 | tf_op jit(solution)/shard_map/all_gather | solution.py:78
  73.9 1.2 copy-start.3
  129.2 2.7 copy-start.1
  132.4 6.2 %copy-start.4 = (bf16[768,1024]{1,0:T(8,128)(2,1)S(1)}, bf16[768,1024]{1,0:T(8,128)(2,1)}, u32[]{:S(2)}) copy-start(bf16[768,1024]{1,0:T(8,128)(2,1)} %copy-done.3) | copy-start | bytes 4718596
  132.4 6.2 %copy-start.7 = (bf16[1024,2048]{1,0:T(8,128)(2,1)S(1)}, bf16[1024,2048]{1,0:T(8,128)(2,1)}, u32[]{:S(2)}) copy-start(bf16[1024,2048]{1,0:T(8,128)(2,1)} %all-gather.6.cloned.1.call-done) | copy-start | bytes 12582916
  136.9 1.8 copy-start.2
  142.5 9.0 %copy-start.5 = (f32[1,1,3]{2,1,0:T(1,128)S(1)}, f32[1,1,3]{2,1,0:T(1,128)}, u32[]{:S(2)}) copy-start(f32[1,1,3]{2,1,0:T(1,128)} %param.13) | copy-start | bytes 40
  142.5 9.0 %copy-start.6 = (s32[1,1,3]{2,1,0:T(1,128)S(1)}, s32[1,1,3]{2,1,0:T(1,128)}, u32[]{:S(2)}) copy-start(s32[1,1,3]{2,1,0:T(1,128)} %param.12) | copy-start | bytes 40
  152.1 153.6 %copy-start.8 = (u32[256]{0:T(256)S(1)}, u32[256]{0:T(256)}, u32[]{:S(2)}) copy-start(u32[256]{0:T(256)} %constant.35) | copy-start | bytes 3076
  298.7 74.0 %all-to-all-start = ((bf16[32,4,2048]{2,1,0:T(4,128)(2,1)}), bf16[32,4,2048]{2,1,0:T(4,128)(2,1)}, u32[]{:S(2)}, u32[]{:S(2)}) async-start(bf16[32,4,2048]{2,1,0:T(4,128)(2,1)} %stack.5), calls=%async_computation | async-start | bytes 1048576 | tf_op jit(solution)/shard_map/all_to_all | solution.py:121
Sparse Core Ops, SparseCore 0:
  9.8 58.3 all-gather.3
  70.0 53.3 all-gather.5
